TPU v7x, 256 devices: a whole 4x4x8 slice. The times are simulated.
256 devices in a mesh: dp: 64 (over z_hi, x, y, core), fsdp: 4 (over z_lo).
Axes of the slice: x: 4, y: 4, z: 8 (z_hi: 2, z_lo: 4; z = z_hi * 4 + z_lo), core: 2. Of those that a mesh axis runs over, the one named last changes fastest.
Arguments:
- student_tiles: bfloat16 [32768, 16, 256], P(('dp', 'fsdp')), may hold values from -6 to 6
- teacher_tiles: bfloat16 [32768, 16, 512], P(('dp', 'fsdp')), may hold values from -6 to 6
- send_list: int32 [64, 4, 128], P('dp', 'fsdp'), may hold values from -1 to 127, as said below
- clip_weight: float32 [32768], P(('dp', 'fsdp')), may hold values from 0.5 to 64, as said below
- kernel_dilated: bfloat16 [1792, 256], P('fsdp'), may hold values from -0.125 to 0.125
- kernel_mix: bfloat16 [256, 256], P('fsdp'), may hold values from -0.375 to 0.375
- kernel_down: bfloat16 [4096, 512], P('fsdp'), may hold values from -0.09375 to 0.09375
- kernel_proj: bfloat16 [512, 1024], P('fsdp'), may hold values from -0.25 to 0.25
- kernel_teacher: bfloat16 [16, 512, 1024], P(None, 'fsdp'), may hold values from -0.0625 to 0.0625
- alpha_one: float32 [256], replicated, may hold values from 0.5 to 2
- alpha_two: float32 [256], replicated, may hold values from 0.5 to 2
- alpha_three: float32 [256], replicated, may hold values from 0.5 to 2
- alpha_teacher: float32 [512], replicated, may hold values from 0.5 to 2
Outputs:
- student_latent: bfloat16 [32768, 2, 1024], P(('dp', 'fsdp'))
- grad_dilated: float32 [458752], P(('dp', 'fsdp'))
- grad_mix: float32 [65536], P(('dp', 'fsdp'))
- grad_down: float32 [2097152], P(('dp', 'fsdp'))
- grad_proj: float32 [524288], P(('dp', 'fsdp'))
Inputs may be any that keep to these rules, and one draw needn't show every extreme that they name: `send_list`: entries d * 2 .. d * 2 + 1 of a device's list go to dp owner d. Each device's tiles 0 .. L - 1 appear exactly once and no other tile appears, for a count L of 2 to 128 drawn per device; on every device one owner receives 2 tiles, and some device has L = 128. `clip_weight`: positive weights.
All inputs are finite; a program needn't handle non-finite values.
Results may differ from a plain program's by a relative error of at most 0.0067.
Values may be sent and summed in bfloat16 or wider, within the bound.
A program may use at most 128 MiB of HBM per device.

v0:
```python
import jax
import jax.numpy as jnp
from jax import lax
from jax.sharding import PartitionSpec as P

DL = 1024
KS = 16
STRIDE = 8
DILATED_TAPS = 7
UNIT_DILATION = 3
TILE_FRAMES = 16
OUTF = 2


def snake(values, alpha_vec):
    widened = values.astype(jnp.float32)
    return widened + jnp.square(jnp.sin(alpha_vec * widened)) / alpha_vec


def snake_slope(values, alpha_vec):
    return 1.0 + jnp.sin(2.0 * alpha_vec * values)


def unfold_strided(frames):
    tile_count = frames.shape[0]
    margin = (KS - STRIDE) // 2
    padded_frames = jnp.pad(frames, ((0, 0), (margin, margin), (0, 0)))
    windows = [
        padded_frames[:, STRIDE * offset : STRIDE * offset + KS, :].reshape(tile_count, -1)
        for offset in range(OUTF)
    ]
    return jnp.stack(windows, axis=1)


def fold_strided(columns, channels):
    tile_count = columns.shape[0]
    margin = (KS - STRIDE) // 2
    padded_len = TILE_FRAMES + 2 * margin
    pieces = columns.reshape(tile_count, OUTF, KS, channels)
    folded = jnp.zeros((tile_count, padded_len, channels), jnp.float32)
    for offset in range(OUTF):
        folded = folded + jnp.pad(
            pieces[:, offset],
            ((0, 0), (STRIDE * offset, padded_len - KS - STRIDE * offset), (0, 0)),
        )
    return folded[:, margin : margin + TILE_FRAMES, :]


def unfold_dilated(frames):
    tile_count = frames.shape[0]
    receptive_length = UNIT_DILATION * (DILATED_TAPS - 1) // 2
    padded_frames = jnp.pad(frames, ((0, 0), (receptive_length, receptive_length), (0, 0)))
    tap_offsets = [
        padded_frames[
            :, UNIT_DILATION * tap_position : UNIT_DILATION * tap_position + TILE_FRAMES, :
        ]
        for tap_position in range(DILATED_TAPS)
    ]
    return jnp.stack(tap_offsets, axis=2).reshape(tile_count * TILE_FRAMES, -1)


def teacher_forward(tiles, kernel_teacher, alpha_teacher):
    tile_count = tiles.shape[0]
    activated = snake(tiles, alpha_teacher).astype(jnp.bfloat16)
    spread = lax.all_to_all(activated, "fsdp", split_axis=2, concat_axis=0, tiled=True)
    flat_kernel = kernel_teacher.reshape(-1, DL)
    columns = unfold_strided(spread).reshape(tile_count * lax.axis_size("fsdp") * OUTF, -1)
    return lax.psum_scatter(
        jnp.dot(columns, flat_kernel, preferred_element_type=jnp.float32).reshape(
            tile_count * lax.axis_size("fsdp"), OUTF, DL
        ),
        "fsdp",
        scatter_dimension=0,
        tiled=True,
    ).astype(jnp.bfloat16)


def student_step(tiles, target, weights, kernels, alphas):
    kernel_dilated, kernel_mix, kernel_down, kernel_proj = kernels
    alpha_one, alpha_two, alpha_three = alphas
    tile_count = tiles.shape[0]
    channels = tiles.shape[2]
    act_one = snake(tiles, alpha_one).astype(jnp.bfloat16)
    dilated = unfold_dilated(act_one)
    hidden = jnp.dot(dilated, kernel_dilated, preferred_element_type=jnp.float32)
    act_two = snake(hidden, alpha_two).astype(jnp.bfloat16)
    residual = tiles.reshape(tile_count * TILE_FRAMES, channels).astype(jnp.float32) + jnp.dot(
        act_two, kernel_mix, preferred_element_type=jnp.float32
    )
    act_three = (
        snake(residual, alpha_three).astype(jnp.bfloat16).reshape(tile_count, TILE_FRAMES, channels)
    )
    strided = unfold_strided(act_three).reshape(tile_count * OUTF, -1)
    student = jnp.dot(strided, kernel_down, preferred_element_type=jnp.float32).astype(jnp.bfloat16)
    predicted = jnp.dot(student, kernel_proj, preferred_element_type=jnp.float32)
    row_weight = jnp.repeat(weights, OUTF)[:, None]
    error = (
        row_weight
        * (predicted - target.reshape(tile_count * OUTF, DL).astype(jnp.float32))
        / (tile_count * OUTF)
    ).astype(jnp.bfloat16)
    grad_proj = jnp.dot(student.T, error, preferred_element_type=jnp.float32)
    back_student = jnp.dot(error, kernel_proj.T, preferred_element_type=jnp.float32).astype(
        jnp.bfloat16
    )
    grad_down = jnp.dot(strided.T, back_student, preferred_element_type=jnp.float32)
    back_columns = jnp.dot(back_student, kernel_down.T, preferred_element_type=jnp.float32).reshape(
        tile_count, OUTF, -1
    )
    back_three = fold_strided(back_columns, channels).reshape(tile_count * TILE_FRAMES, channels)
    back_residual = (back_three * snake_slope(residual, alpha_three)).astype(jnp.bfloat16)
    grad_mix = jnp.dot(act_two.T, back_residual, preferred_element_type=jnp.float32)
    back_hidden = (
        jnp.dot(back_residual, kernel_mix.T, preferred_element_type=jnp.float32)
        * snake_slope(hidden, alpha_two)
    ).astype(jnp.bfloat16)
    grad_dilated = jnp.dot(dilated.T, back_hidden, preferred_element_type=jnp.float32)
    latent = predicted.astype(jnp.bfloat16).reshape(tile_count, OUTF, DL)
    return (
        latent,
        (
            grad_dilated.reshape(-1),
            grad_mix.reshape(-1),
            grad_down.reshape(-1),
            grad_proj.reshape(-1),
        ),
    )


def on_device(
    student_tiles,
    teacher_tiles,
    send_list,
    clip_weight,
    kernel_dilated,
    kernel_mix,
    kernel_down,
    kernel_proj,
    kernel_teacher,
    alpha_one,
    alpha_two,
    alpha_three,
    alpha_teacher,
):
    routes = send_list.reshape(-1)
    live_rows = (routes >= 0)[:, None, None]
    picked = jnp.maximum(routes, 0)

    def packed(values):
        return jnp.where(live_rows, jnp.take(values, picked, axis=0), jnp.zeros((), values.dtype))

    student_part, teacher_part = (
        lax.all_to_all(packed(student_tiles), "dp", split_axis=0, concat_axis=0, tiled=True),
        lax.all_to_all(packed(teacher_tiles), "dp", split_axis=0, concat_axis=0, tiled=True),
    )
    target = teacher_forward(teacher_part, kernel_teacher, alpha_teacher)
    kernels = (
        lax.all_gather(kernel_dilated, "fsdp", axis=0, tiled=True),
        lax.all_gather(kernel_mix, "fsdp", axis=0, tiled=True),
        lax.all_gather(kernel_down, "fsdp", axis=0, tiled=True),
        lax.all_gather(kernel_proj, "fsdp", axis=0, tiled=True),
    )
    latent, gradients = student_step(
        student_part, target, clip_weight, kernels, (alpha_one, alpha_two, alpha_three)
    )
    gradients = (
        lax.psum_scatter(gradients[0], ("dp", "fsdp"), scatter_dimension=0, tiled=True),
        lax.psum_scatter(gradients[1], ("dp", "fsdp"), scatter_dimension=0, tiled=True),
        lax.psum_scatter(gradients[2], ("dp", "fsdp"), scatter_dimension=0, tiled=True),
        lax.psum_scatter(gradients[3], ("dp", "fsdp"), scatter_dimension=0, tiled=True),
    )
    return (latent, gradients[0], gradients[1], gradients[2], gradients[3])


def solution(mesh):
    placed = (
        P(("dp", "fsdp"), None, None),
        P(("dp", "fsdp"), None, None),
        P("dp", "fsdp", None),
        P(("dp", "fsdp")),
        P("fsdp", None),
        P("fsdp", None),
        P("fsdp", None),
        P("fsdp", None),
        P(None, "fsdp", None),
        P(),
        P(),
        P(),
        P(),
    )
    return jax.shard_map(
        on_device,
        mesh=mesh,
        in_specs=placed,
        out_specs=(
            P(("dp", "fsdp"), None, None),
            P(("dp", "fsdp")),
            P(("dp", "fsdp")),
            P(("dp", "fsdp")),
            P(("dp", "fsdp")),
        ),
        check_vma=False,
    )
```

profile of v0, /device:TPU:8, one launch (start us, length us, event | category | flops | bytes accessed | tf_op | source)
XLA Modules:
  0.0 759.4 jit_solution(11630443974876374161)
XLA Ops:
  8.8 2.0 gather_fusion.1
  10.8 3.0 select_select_fusion
  13.8 14.7 %all-to-all-start.1 = ((bf16[128,16,512]{2,1,0:T(8,128)(2,1)}), bf16[128,16,512]{2,1,0:T(8,128)(2,1)S(1)}, u32[]{:S(2)}, u32[]{:S(2)}) async-start(bf16[128,16,512]{2,1,0:T(8,128)(2,1)} %select_select_fusion), calls=%async_computation.1 | async-start | bytes 4194304 | tf_op jit(solution)/shard_map/all_to_all | solution.py:154
  29.3 46.7 %all-to-all-done.1 = bf16[128,16,512]{2,1,0:T(8,128)(2,1)S(1)} async-done(((bf16[128,16,512]{2,1,0:T(8,128)(2,1)}), bf16[128,16,512]{2,1,0:T(8,128)(2,1)S(1)}, u32[]{:S(2)}, u32[]{:S(2)}) %all-to-all-start.1) | async-done | bytes 2097184 | tf_op jit(solution)/shard_map/all_to_all | solution.py:154
  75.9 15.0 %fusion.3 = bf16[128,16,512]{2,1,0:T(8,128)(2,1)} fusion(bf16[128,16,512]{2,1,0:T(8,128)(2,1)S(1)} %all-to-all-done.1, f32[512]{0:T(512)S(1)} %copy-done.13), kind=kLoop, calls=%fused_computation.13 | loop fusion | flops 6291456 | bytes 4196352 | tf_op jit(solution)/shard_map/convert_element_type | solution.py:64
  91.0 4.2 copy.52
  95.2 93.7 %all_to_all.28 = bf16[128,16,512]{0,1,2:T(8,128)(2,1)} all-to-all(bf16[128,16,512]{0,1,2:T(8,128)(2,1)S(1)} %copy.52), channel_id=1, replica_groups=mesh['dp'=64,'fsdp'=4] {'fsdp'}, dimensions={2} | all-to-all | bytes 4194304 | tf_op jit(solution)/shard_map/all_to_all | solution.py:65
  189.0 5.1 copy.53
  194.0 5.3 pad_slice_fusion.7
  199.4 4.1 stack_reshape.15
  203.5 2.3 stack_reshape.14
  205.8 10.0 %fusion.4 = f32[512,2,1024]{2,0,1:T(8,128)} fusion(bf16[2048,1024,1]{1,0,2:T(8,128)(2,1)} %bitcast.109, bf16[512,1,2048]{2,0,1:T(8,128)(2,1)} %stack_reshape.15, bf16[512,1,2048]{2,0,1:T(8,128)(2,1)} %stack_reshape.14), kind=kOutput, calls=%fused_computation.14 | convolution fusion | flops 4297064448 | bytes 12582912 | tf_op jit(solution)/shard_map/dot_general | solution.py:69
  217.7 1.5 select_select_fusion.1
  219.2 11.7 %all-to-all-start = ((bf16[128,16,256]{2,1,0:T(8,128)(2,1)}), bf16[128,16,256]{2,1,0:T(8,128)(2,1)S(1)}, u32[]{:S(2)}, u32[]{:S(2)}) async-start(bf16[128,16,256]{2,1,0:T(8,128)(2,1)} %select_select_fusion.1), calls=%async_computation | async-start | bytes 2097152 | tf_op jit(solution)/shard_map/all_to_all | solution.py:153
  232.0 56.0 %all_gather.13 = bf16[256,256]{1,0:T(8,128)(2,1)S(1)} all-gather(bf16[64,256]{1,0:T(8,128)(2,1)S(1)} %copy-done.11), channel_id=1, replica_groups=mesh['dp'=64,'fsdp'=4] {'fsdp'}, dimensions={0}, use_global_device_ids=true | all-gather | bytes 163840 | tf_op jit(solution)/shard_map/all_gather | solution.py:159
  288.0 34.1 %all_gather.12 = bf16[1792,256]{1,0:T(8,128)(2,1)} all-gather(bf16[448,256]{1,0:T(8,128)(2,1)S(1)} %copy-done.10), channel_id=1, replica_groups=mesh['dp'=64,'fsdp'=4] {'fsdp'}, dimensions={0}, use_global_device_ids=true | all-gather | bytes 1146880 | tf_op jit(solution)/shard_map/all_gather | solution.py:158
  322.1 7.3 add_convert_fusion.2
  330.5 1.5 fusion.13
  332.0 1.4 fusion.15
  333.4 7.9 %bitcast_dynamic-update-slice_fusion = bf16[128,16,7,256]{3,1,0,2:T(8,128)(2,1)} fusion(bf16[128,16,7,256]{3,1,0,2:T(8,128)(2,1)} %fusion.15, f32[256]{0:T(256)S(1)} %copy-done.12, bf16[128,16,256]{2,1,0:T(8,128)(2,1)S(1)} %all-to-all-done), kind=kLoop, calls=%fused_computation.53 | loop fusion | flops 3145728 | bytes 2098176
  341.3 1.4 fusion.17
  342.7 1.5 fusion.19
  345.3 14.4 %copy.49 = bf16[128,16,7,256]{3,2,1,0:T(8,128)(2,1)} copy(bf16[128,16,7,256]{3,1,0,2:T(8,128)(2,1)} %fusion.21) | data formatting | bytes 14680064 | tf_op jit(solution)/shard_map/stack | solution.py:59
  359.8 7.2 copy.59
  367.0 2.1 fusion.26
  369.9 15.2 %add_convert_fusion = (bf16[2048,256]{1,0:T(8,128)(2,1)S(1)}, f32[2048,256]{1,0:T(8,128)}) fusion(f32[256]{0:T(256)S(1)} %copy-done.14, bf16[256,256]{1,0:T(8,128)(2,1)S(1)} %all_gather.13, f32[2048,256]{1,0:T(8,128)S(1)} %fusion.26, f32[256]{0:T(256)S(1)} %copy-done.15, bf16[2048,256]{1,0:T(8,128)(2,1)S(1)} %bitcast.98), kind=kOutput, calls=%fused_computation.31 | convolution fusion | flops 274726912 | bytes 6424576 | tf_op jit(solution)/shard_map/dot_general | solution.py:87
  386.6 4.0 copy.51
  390.6 2.9 reshape.89
  393.5 3.4 convolution_convert_fusion.1
  397.0 1.3 convert_convert_fusion
  398.3 1.8 copy.54
  400.1 1.9 reshape.98
  402.1 2.5 multiply_convert_fusion
  404.6 1.8 convolution_bitcast_fusion.1
  406.9 4.5 convolution_bitcast_fusion
  411.5 1.3 fusion.27
  412.7 1.7 copy.60
  416.6 7.2 fusion.9
  423.8 7.6 %convolution_bitcast_fusion.3 = f32[32,2,8,128]{3,2,1,0:T(8,128)S(1)} fusion(bf16[2048,256]{1,0:T(8,128)(2,1)S(1)} %fusion.9, f32[2048,256]{1,0:T(8,128)S(1)} %copy-done.18, f32[256]{0:T(256)S(1)} %copy-done.15), kind=kOutput, calls=%fused_computation.40 | convolution fusion | flops 271056896 | bytes 3408896 | tf_op jit(solution)/shard_map/dot_general | solution.py:112
  431.5 12.2 %convolution_bitcast_fusion.2 = f32[224,2,8,128]{3,2,1,0:T(8,128)S(1)} fusion(bf16[2048,1792]{1,0:T(8,128)(2,1)} %bitcast.104, bf16[2048,256]{1,0:T(8,128)(2,1)S(1)} %fusion.9, bf16[256,256]{1,0:T(8,128)(2,1)S(1)} %all_gather.13, f32[2048,256]{1,0:T(8,128)} %copy-done.17, f32[256]{0:T(256)S(1)} %broadcast_multiply_fusion), kind=kOutput, calls=%fused_computation.37 | convolution fusion | flops 2149580800 | bytes 12452864 | tf_op jit(solution)/shard_map/dot_general | solution.py:117
  443.7 2.2 copy.61
  446.7 9.0 %copy.63 = f32[512,4,8,128]{3,1,2,0:T(4,128)} copy(f32[512,4,8,128]{3,2,1,0:T(8,128)} %convolution_bitcast_fusion) | data formatting | bytes 16777216
  455.7 1.8 copy.64
  459.5 287.5 %all-reduce.12.cloned.1.call-done = (f32[458752]{0:T(1024)}, f32[65536]{0:T(1024)}, f32[2097152]{0:T(1024)}, f32[524288]{0:T(1024)}) async-done(((f32[458752]{0:T(1024)}, f32[65536]{0:T(1024)}, f32[2097152]{0:T(1024)}, f32[524288]{0:T(1024)}), (f32[458752]{0:T(1024)}, f32[65536]{0:T(1024)}, f32[2097152]{0:T(1024)}, f32[524288]{0:T(1024)})) %all-reduce.12.cloned.1.call-update) | async-done | bytes 12582928
  747.1 1.4 dynamic-slice
  748.5 1.3 dynamic-slice.1
  749.8 1.4 dynamic-slice.2
  751.2 1.3 dynamic-slice.3
  (68 shorter events, 15.4 us)
Async XLA Ops:
  7.2 1.6 copy-start
  13.8 62.2 %copy-start.13 = (f32[512]{0:T(512)S(1)}, f32[512]{0:T(512)}, u32[]{:S(2)}) copy-start(f32[512]{0:T(512)} %param.25) | copy-start | bytes 6148
  13.8 62.2 %all-to-all-start.1 = ((bf16[128,16,512]{2,1,0:T(8,128)(2,1)}), bf16[128,16,512]{2,1,0:T(8,128)(2,1)S(1)}, u32[]{:S(2)}, u32[]{:S(2)}) async-start(bf16[128,16,512]{2,1,0:T(8,128)(2,1)} %select_select_fusion), calls=%async_computation.1 | async-start | bytes 4194304 | tf_op jit(solution)/shard_map/all_to_all | solution.py:154
  28.5 365.0 %all-gather.3.cloned.1.call-start = ((), (), s32[]{:S(2)}) async-start(), calls=%async_computation.4 | async-start | bytes 5242880 | tf_op jit(solution)/shard_map/all_gather | solution.py:160
  29.2 367.8 %reduce-scatter.2.cloned.1.call-start = ((), (), s32[]{:S(2)}) async-start(), calls=%async_computation.6 | async-start | bytes 5242880 | tf_op jit(solution)/shard_map/reduce_scatter | solution.py:68
  215.8 1.2 copy-start.8
  217.7 14.1 %copy-start.16 = (f32[128]{0:T(128)S(1)}, f32[128]{0:T(128)}, u32[]{:S(2)}) copy-start(f32[128]{0:T(128)} %param.16) | copy-start | bytes 1540
  217.7 14.3 %copy-start.11 = (bf16[64,256]{1,0:T(8,128)(2,1)S(1)}, bf16[64,256]{1,0:T(8,128)(2,1)}, u32[]{:S(2)}) copy-start(bf16[64,256]{1,0:T(8,128)(2,1)} %param.18) | copy-start | bytes 98308
  217.7 70.3 %copy-start.14 = (f32[256]{0:T(256)S(1)}, f32[256]{0:T(256)}, u32[]{:S(2)}) copy-start(f32[256]{0:T(256)} %param.24) | copy-start | bytes 3076
  217.7 70.3 %copy-start.15 = (f32[256]{0:T(256)S(1)}, f32[256]{0:T(256)}, u32[]{:S(2)}) copy-start(f32[256]{0:T(256)} %param.23) | copy-start | bytes 3076
  217.7 70.3 %copy-start.10 = (bf16[448,256]{1,0:T(8,128)(2,1)S(1)}, bf16[448,256]{1,0:T(8,128)(2,1)}, u32[]{:S(2)}) copy-start(bf16[448,256]{1,0:T(8,128)(2,1)} %param.17) | copy-start | bytes 688132
  219.2 102.9 %copy-start.12 = (f32[256]{0:T(256)S(1)}, f32[256]{0:T(256)}, u32[]{:S(2)}) copy-start(f32[256]{0:T(256)} %param.22) | copy-start | bytes 3076
  219.2 102.8 %all-to-all-start = ((bf16[128,16,256]{2,1,0:T(8,128)(2,1)}), bf16[128,16,256]{2,1,0:T(8,128)(2,1)S(1)}, u32[]{:S(2)}, u32[]{:S(2)}) async-start(bf16[128,16,256]{2,1,0:T(8,128)(2,1)} %select_select_fusion.1), calls=%async_computation | async-start | bytes 2097152 | tf_op jit(solution)/shard_map/all_to_all | solution.py:153
  230.9 171.1 %all-gather.5.cloned.1.call-start = ((), (), s32[]{:S(2)}) async-start(), calls=%async_computation.5 | async-start | bytes 1310720 | tf_op jit(solution)/shard_map/all_gather | solution.py:161
  231.7 515.4 %all-reduce.12.cloned.1.call-start = ((), (), s32[]{:S(2)}) async-start(), calls=%async_computation.7 | async-start | bytes 25165824
  359.8 7.2 copy-start.9
  366.9 2.9 copy-start.3
  369.9 15.2 %copy-start.17 = (f32[2048,256]{1,0:T(8,128)}, f32[2048,256]{1,0:T(8,128)S(1)}, u32[]{:S(2)}) copy-start(f32[2048,256]{1,0:T(8,128)S(1)} %fusion.26) | copy-start | bytes 6291460
  404.6 1.8 copy-start.4
  406.9 4.6 copy-start.5
  415.0 1.6 copy-start.7
  416.6 7.2 copy-start.18
  446.7 9.0 %copy-start.2 = (f32[64,8,8,128]{3,2,1,0:T(8,128)S(1)}, f32[64,8,8,128]{3,2,1,0:T(8,128)}, u32[]{:S(2)}) copy-start(f32[64,8,8,128]{3,2,1,0:T(8,128)} %convolution_bitcast_fusion.1) | copy-start | bytes 6291460
  457.5 1.0 copy-start.6
  457.5 294.9 %copy-start.1 = (bf16[128,16,512]{2,1,0:T(8,128)(2,1)S(1)}, bf16[128,16,512]{2,1,0:T(8,128)(2,1)}, u32[]{:S(2)}) copy-start(bf16[128,16,512]{2,1,0:T(8,128)(2,1)} %param.14) | copy-start | bytes 6291460
Sparse Core Ops, SparseCore 0:
  31.1 111.8 all-gather.2
  215.9 121.1 reduce-scatter.1
  339.0 33.9 all-gather.4
  457.7 289.3 all-reduce.11
where the time goes:
time: 769 us; the launch traced here: 759 us
  waiting for transfers between devices  336 us (44%)
  blocking collectives  184 us (24%)
  local copies, waits for them, and re-layouts  92.4 us (12%)
  matrix products  61.1 us (8%)
  other arithmetic  45.3 us (6%)
  starting transfers between devices  26.6 us (3%)
  between operations  14.5 us (2%)
    unnamed x5, waiting for transfers between devices  289 us
    all_to_all x1, blocking collectives, teacher_forward(): lax.all_to_all(activated, 'fsdp', split_axis=2, concat_axis=0, tiled=True)  93.7 us
    all_gather x1, blocking collectives, on_device(): lax.all_gather(kernel_mix, 'fsdp', axis=0, tiled=True)  56 us
    all_to_all x1, waiting for transfers between devices, on_device(): lax.all_to_all(packed(teacher_tiles), 'dp', split_axis=0, concat_axis=0,...  46.7 us
    unnamed x53, local copies, waits for them, and re-layouts  39.3 us
    all_gather x1, blocking collectives, on_device(): lax.all_gather(kernel_dilated, 'fsdp', axis=0, tiled=True)  34.1 us
    another operation x2, local copies, waits for them, and re-layouts, unfold_dilated(): return jnp.stack(tap_offsets, axis=2).reshape(tile_count * TILE_FRAMES, -1)  15.6 us
  transfers between devices with their start and end apart: 6, of which 2 were waited for; matrix products, arithmetic and copies ran while one was open for 17% of the time, Pallas kernels for 0%

commit v1 on v0

--- a/solution.py
+++ b/solution.py
@@ -156,7 +156,9 @@
     target = teacher_forward(teacher_part, kernel_teacher, alpha_teacher)
     kernels = (
         lax.all_gather(kernel_dilated, "fsdp", axis=0, tiled=True),
-        lax.all_gather(kernel_mix, "fsdp", axis=0, tiled=True),
+        jnp.concatenate(
+            lax.all_to_all(jnp.stack([kernel_mix] * lax.axis_size("fsdp")), "fsdp", 0, 0), axis=0
+        ),
         lax.all_gather(kernel_down, "fsdp", axis=0, tiled=True),
         lax.all_gather(kernel_proj, "fsdp", axis=0, tiled=True),
     )

time: 769 us -> 765 us (level)
  blocking collectives: 184 us -> 169 us
    all_gather x1 -> x0, blocking collectives: 56 us -> none  [on_device(): lax.all_gather(kernel_mix, 'fsdp', axis=0, tiled=True)]
    all_gather x1, blocking collectives: 34.1 us -> 74.8 us  [on_device(): lax.all_gather(kernel_dilated, 'fsdp', axis=0, tiled=True)]
    unnamed x53 -> x51, local copies, waits for them, and re-layouts: 39.3 us -> 41.6 us
  transfers between devices with their start and end apart: 6 -> 7, of which waited for: 2 -> 2; matrix products, arithmetic and copies ran while one was open for 17% -> 18% of each run, Pallas kernels for 0% -> 0%
where the time goes in v1:
time: 765 us; the launch traced here: 755 us
  waiting for transfers between devices  337 us (44%)
  blocking collectives  169 us (22%)
  local copies, waits for them, and re-layouts  95.5 us (12%)
  matrix products  63.8 us (8%)
  other arithmetic  45.3 us (6%)
  starting transfers between devices  30.5 us (4%)
  between operations  14.5 us (2%)
    unnamed x5, waiting for transfers between devices  290 us
    all_to_all x1, blocking collectives, teacher_forward(): lax.all_to_all(activated, 'fsdp', split_axis=2, concat_axis=0, tiled=True)  93.7 us
    all_gather x1, blocking collectives, on_device(): lax.all_gather(kernel_dilated, 'fsdp', axis=0, tiled=True)  74.8 us
    all_to_all x1, waiting for transfers between devices, on_device(): lax.all_to_all(packed(teacher_tiles), 'dp', split_axis=0, concat_axis=0,...  46.7 us
    unnamed x51, local copies, waits for them, and re-layouts  41.6 us
    dot_general x1, matrix products, student_step(): jnp.dot(act_two, kernel_mix, preferred_element_type=jnp.float32)  16.5 us
    another operation x2, local copies, waits for them, and re-layouts, unfold_dilated(): return jnp.stack(tap_offsets, axis=2).reshape(tile_count * TILE_FRAMES, -1)  15.6 us
  transfers between devices with their start and end apart: 7, of which 2 were waited for; matrix products, arithmetic and copies ran while one was open for 18% of the time, Pallas kernels for 0%

profile of v1, /device:TPU:8, one launch (start us, length us, event | category | flops | bytes accessed | tf_op | source)
XLA Modules:
  0.0 754.9 jit_solution(17764694372731030763)
XLA Ops:
  8.8 2.0 gather_fusion.1
  10.8 3.0 select_select_fusion
  13.8 14.7 %all-to-all-start.2 = ((bf16[128,16,512]{2,1,0:T(8,128)(2,1)}), bf16[128,16,512]{2,1,0:T(8,128)(2,1)S(1)}, u32[]{:S(2)}, u32[]{:S(2)}) async-start(bf16[128,16,512]{2,1,0:T(8,128)(2,1)} %select_select_fusion), calls=%async_computation.2 | async-start | bytes 4194304 | tf_op jit(solution)/shard_map/all_to_all | solution.py:154
  29.3 46.7 %all-to-all-done.2 = bf16[128,16,512]{2,1,0:T(8,128)(2,1)S(1)} async-done(((bf16[128,16,512]{2,1,0:T(8,128)(2,1)}), bf16[128,16,512]{2,1,0:T(8,128)(2,1)S(1)}, u32[]{:S(2)}, u32[]{:S(2)}) %all-to-all-start.2) | async-done | bytes 2097184 | tf_op jit(solution)/shard_map/all_to_all | solution.py:154
  76.0 15.0 %fusion.3 = bf16[128,16,512]{2,1,0:T(8,128)(2,1)} fusion(bf16[128,16,512]{2,1,0:T(8,128)(2,1)S(1)} %all-to-all-done.2, f32[512]{0:T(512)S(1)} %copy-done.13), kind=kLoop, calls=%fused_computation.13 | loop fusion | flops 6291456 | bytes 4196352 | tf_op jit(solution)/shard_map/convert_element_type | solution.py:64
  91.0 4.2 copy.52
  95.2 93.7 %all_to_all.33 = bf16[128,16,512]{0,1,2:T(8,128)(2,1)} all-to-all(bf16[128,16,512]{0,1,2:T(8,128)(2,1)S(1)} %copy.52), channel_id=1, replica_groups=mesh['dp'=64,'fsdp'=4] {'fsdp'}, dimensions={2} | all-to-all | bytes 4194304 | tf_op jit(solution)/shard_map/all_to_all | solution.py:65
  189.0 5.1 copy.53
  194.1 5.3 pad_slice_fusion.7
  199.4 4.2 stack_reshape.15
  203.6 2.3 stack_reshape.14
  205.9 10.0 %fusion.4 = f32[512,2,1024]{2,0,1:T(8,128)} fusion(bf16[2048,1024,1]{1,0,2:T(8,128)(2,1)} %bitcast.112, bf16[512,1,2048]{2,0,1:T(8,128)(2,1)} %stack_reshape.15, bf16[512,1,2048]{2,0,1:T(8,128)(2,1)} %stack_reshape.14), kind=kOutput, calls=%fused_computation.14 | convolution fusion | flops 4297064448 | bytes 12582912 | tf_op jit(solution)/shard_map/dot_general | solution.py:69
  217.8 1.5 select_select_fusion.1
  219.3 11.7 %all-to-all-start = ((bf16[128,16,256]{2,1,0:T(8,128)(2,1)}), bf16[128,16,256]{2,1,0:T(8,128)(2,1)S(1)}, u32[]{:S(2)}, u32[]{:S(2)}) async-start(bf16[128,16,256]{2,1,0:T(8,128)(2,1)} %select_select_fusion.1), calls=%async_computation | async-start | bytes 2097152 | tf_op jit(solution)/shard_map/all_to_all | solution.py:153
  232.0 74.8 %all_gather.9 = bf16[1792,256]{1,0:T(8,128)(2,1)} all-gather(bf16[448,256]{1,0:T(8,128)(2,1)S(1)} %copy-done.10), channel_id=1, replica_groups=mesh['dp'=64,'fsdp'=4] {'fsdp'}, dimensions={0}, use_global_device_ids=true | all-gather | bytes 1146880 | tf_op jit(solution)/shard_map/all_gather | solution.py:158
  307.5 4.0 all-to-all-start.1
  311.5 7.3 add_convert_fusion.2
  319.9 1.5 fusion.13
  321.4 1.4 fusion.15
  322.8 7.8 %bitcast_dynamic-update-slice_fusion = bf16[128,16,7,256]{3,1,0,2:T(8,128)(2,1)} fusion(bf16[128,16,7,256]{3,1,0,2:T(8,128)(2,1)} %fusion.15, f32[256]{0:T(256)S(1)} %copy-done.12, bf16[128,16,256]{2,1,0:T(8,128)(2,1)S(1)} %all-to-all-done), kind=kLoop, calls=%fused_computation.53 | loop fusion | flops 3145728 | bytes 2098176
  330.7 1.4 fusion.17
  332.1 1.5 fusion.19
  334.7 14.5 %copy.49 = bf16[128,16,7,256]{3,2,1,0:T(8,128)(2,1)} copy(bf16[128,16,7,256]{3,1,0,2:T(8,128)(2,1)} %fusion.21) | data formatting | bytes 14680064 | tf_op jit(solution)/shard_map/stack | solution.py:59
  349.2 7.3 copy.59
  356.6 2.9 copy-done.3
  359.5 3.5 fusion.26
  363.0 16.5 %add_convert_fusion = (bf16[2048,256]{1,0:T(8,128)(2,1)S(1)}, f32[2048,256]{1,0:T(8,128)}) fusion(f32[256]{0:T(256)S(1)} %copy-done.14, bf16[256,256]{1,0:T(8,128)(2,1)S(1)} %bitcast.110, f32[2048,256]{1,0:T(8,128)} %fusion.26, f32[256]{0:T(256)S(1)} %copy-done.15, bf16[2048,256]{1,0:T(8,128)(2,1)S(1)} %bitcast.99), kind=kOutput, calls=%fused_computation.31 | convolution fusion | flops 274726912 | bytes 6424576 | tf_op jit(solution)/shard_map/dot_general | solution.py:87
  381.1 4.0 copy.51
  385.1 2.9 reshape.95
  388.0 3.4 convolution_convert_fusion.1
  391.5 1.3 convert_convert_fusion
  392.8 1.8 copy.54
  394.6 1.9 reshape.104
  396.6 2.5 multiply_convert_fusion
  399.0 1.8 convolution_bitcast_fusion.1
  401.4 4.5 convolution_bitcast_fusion
  407.2 1.7 copy.60
  411.1 7.2 fusion.9
  418.3 7.6 %convolution_bitcast_fusion.3 = f32[32,2,8,128]{3,2,1,0:T(8,128)S(1)} fusion(bf16[2048,256]{1,0:T(8,128)(2,1)S(1)} %fusion.9, f32[2048,256]{1,0:T(8,128)S(1)} %copy-done.17, f32[256]{0:T(256)S(1)} %copy-done.15), kind=kOutput, calls=%fused_computation.40 | convolution fusion | flops 271056896 | bytes 3408896 | tf_op jit(solution)/shard_map/dot_general | solution.py:112
  425.9 12.2 %convolution_bitcast_fusion.2 = f32[224,2,8,128]{3,2,1,0:T(8,128)S(1)} fusion(bf16[2048,1792]{1,0:T(8,128)(2,1)} %bitcast.105, bf16[2048,256]{1,0:T(8,128)(2,1)S(1)} %fusion.9, bf16[256,256]{1,0:T(8,128)(2,1)S(1)} %bitcast.111, f32[2048,256]{1,0:T(8,128)} %fusion.26, f32[256]{0:T(256)S(1)} %broadcast_multiply_fusion), kind=kOutput, calls=%fused_computation.37 | convolution fusion | flops 2149580800 | bytes 12452864 | tf_op jit(solution)/shard_map/dot_general | solution.py:117
  438.1 2.2 copy.61
  441.2 9.0 %copy.63 = f32[512,4,8,128]{3,1,2,0:T(4,128)} copy(f32[512,4,8,128]{3,2,1,0:T(8,128)} %convolution_bitcast_fusion) | data formatting | bytes 16777216
  450.2 1.8 copy.64
  454.0 288.7 %all-reduce.12.cloned.1.call-done = (f32[458752]{0:T(1024)}, f32[65536]{0:T(1024)}, f32[2097152]{0:T(1024)}, f32[524288]{0:T(1024)}) async-done(((f32[458752]{0:T(1024)}, f32[65536]{0:T(1024)}, f32[2097152]{0:T(1024)}, f32[524288]{0:T(1024)}), (f32[458752]{0:T(1024)}, f32[65536]{0:T(1024)}, f32[2097152]{0:T(1024)}, f32[524288]{0:T(1024)})) %all-reduce.12.cloned.1.call-update) | async-done | bytes 12582928
  742.7 1.4 dynamic-slice
  744.0 1.3 dynamic-slice.1
  745.4 1.4 dynamic-slice.2
  746.7 1.3 dynamic-slice.3
  (68 shorter events, 16.5 us)
Async XLA Ops:
  7.2 1.6 copy-start
  13.8 62.2 %copy-start.13 = (f32[512]{0:T(512)S(1)}, f32[512]{0:T(512)}, u32[]{:S(2)}) copy-start(f32[512]{0:T(512)} %param.25) | copy-start | bytes 6148
  13.8 62.2 %all-to-all-start.2 = ((bf16[128,16,512]{2,1,0:T(8,128)(2,1)}), bf16[128,16,512]{2,1,0:T(8,128)(2,1)S(1)}, u32[]{:S(2)}, u32[]{:S(2)}) async-start(bf16[128,16,512]{2,1,0:T(8,128)(2,1)} %select_select_fusion), calls=%async_computation.2 | async-start | bytes 4194304 | tf_op jit(solution)/shard_map/all_to_all | solution.py:154
  28.5 359.5 %all-gather.3.cloned.1.call-start = ((), (), s32[]{:S(2)}) async-start(), calls=%async_computation.5 | async-start | bytes 5242880 | tf_op jit(solution)/shard_map/all_gather | solution.py:162
  29.2 362.2 %reduce-scatter.2.cloned.1.call-start = ((), (), s32[]{:S(2)}) async-start(), calls=%async_computation.7 | async-start | bytes 5242880 | tf_op jit(solution)/shard_map/reduce_scatter | solution.py:68
  215.8 1.2 copy-start.8
  217.7 14.0 %copy-start.16 = (f32[128]{0:T(128)S(1)}, f32[128]{0:T(128)}, u32[]{:S(2)}) copy-start(f32[128]{0:T(128)} %param.16) | copy-start | bytes 1540
  217.7 14.3 %copy-start.14 = (f32[256]{0:T(256)S(1)}, f32[256]{0:T(256)}, u32[]{:S(2)}) copy-start(f32[256]{0:T(256)} %param.24) | copy-start | bytes 3076
  217.7 14.3 %copy-start.15 = (f32[256]{0:T(256)S(1)}, f32[256]{0:T(256)}, u32[]{:S(2)}) copy-start(f32[256]{0:T(256)} %param.23) | copy-start | bytes 3076
  217.7 14.3 %copy-start.10 = (bf16[448,256]{1,0:T(8,128)(2,1)S(1)}, bf16[448,256]{1,0:T(8,128)(2,1)}, u32[]{:S(2)}) copy-start(bf16[448,256]{1,0:T(8,128)(2,1)} %param.17) | copy-start | bytes 688132
  219.3 87.5 %copy-start.11 = (bf16[64,256]{1,0:T(8,128)(2,1)S(1)}, bf16[64,256]{1,0:T(8,128)(2,1)}, u32[]{:S(2)}) copy-start(bf16[64,256]{1,0:T(8,128)(2,1)} %param.18) | copy-start | bytes 98308
  219.3 92.2 %copy-start.12 = (f32[256]{0:T(256)S(1)}, f32[256]{0:T(256)}, u32[]{:S(2)}) copy-start(f32[256]{0:T(256)} %param.22) | copy-start | bytes 3076
  219.3 87.5 %all-to-all-start = ((bf16[128,16,256]{2,1,0:T(8,128)(2,1)}), bf16[128,16,256]{2,1,0:T(8,128)(2,1)S(1)}, u32[]{:S(2)}, u32[]{:S(2)}) async-start(bf16[128,16,256]{2,1,0:T(8,128)(2,1)} %select_select_fusion.1), calls=%async_computation | async-start | bytes 2097152 | tf_op jit(solution)/shard_map/all_to_all | solution.py:153
  231.0 165.6 %all-gather.5.cloned.1.call-start = ((), (), s32[]{:S(2)}) async-start(), calls=%async_computation.6 | async-start | bytes 1310720 | tf_op jit(solution)/shard_map/all_gather | solution.py:163
  307.5 55.5 %all-to-all-start.1 = ((bf16[4,64,256]{2,1,0:T(8,128)(2,1)}), bf16[4,64,256]{2,1,0:T(8,128)(2,1)S(1)}, u32[]{:S(2)}, u32[]{:S(2)}) async-start(bf16[4,64,256]{2,1,0:T(8,128)(2,1)} %stack.45), calls=%async_computation.1 | async-start | bytes 262144 | tf_op jit(solution)/shard_map/all_to_all | solution.py:160
  311.5 431.2 %all-reduce.12.cloned.1.call-start = ((), (), s32[]{:S(2)}) async-start(), calls=%async_computation.8 | async-start | bytes 25165824
  349.2 10.3 %copy-start.9 = (bf16[1792,256]{1,0:T(8,128)(2,1)S(1)}, bf16[1792,256]{1,0:T(8,128)(2,1)}, u32[]{:S(2)}) copy-start(bf16[1792,256]{1,0:T(8,128)(2,1)} %all_gather.9) | copy-start | bytes 2752516
  356.6 2.9 copy-start.3
  399.0 1.8 copy-start.4
  401.4 4.6 copy-start.5
  409.5 1.6 copy-start.7
  411.1 7.2 copy-start.17
  441.2 9.0 %copy-start.2 = (f32[64,8,8,128]{3,2,1,0:T(8,128)S(1)}, f32[64,8,8,128]{3,2,1,0:T(8,128)}, u32[]{:S(2)}) copy-start(f32[64,8,8,128]{3,2,1,0:T(8,128)} %convolution_bitcast_fusion.1) | copy-start | bytes 6291460
  452.0 1.0 copy-start.6
  452.0 296.1 %copy-start.1 = (bf16[128,16,512]{2,1,0:T(8,128)(2,1)S(1)}, bf16[128,16,512]{2,1,0:T(8,128)(2,1)}, u32[]{:S(2)}) copy-start(bf16[128,16,512]{2,1,0:T(8,128)(2,1)} %param.14) | copy-start | bytes 6291460
Sparse Core Ops, SparseCore 0:
  31.1 111.8 all-gather.2
  216.0 121.1 reduce-scatter.1
  339.0 33.9 all-gather.4
  452.1 290.5 all-reduce.11
